TPU v7x, 32 devices: a whole 2x2x4 slice. The times are simulated.
32 devices in a mesh: sp: 16 (over z, y, x), pb: 2 (over core).
Axes of the slice: x: 2, y: 2, z: 4, core: 2. Of those that a mesh axis runs over, the one named last changes fastest.
Arguments:
- amplitudes: bfloat16 [40, 1024, 1024], P('pb', 'sp'), may hold values from -6 to 6
- virtuals: bfloat16 [1400, 1024], replicated, may hold values from -0.375 to 0.375
- energies: float32 [1024], replicated, may hold values from 0.02 to 0.2
- integrals: bfloat16 [2048, 2048], P('sp'), may hold values from -0.125 to 0.125
- screened: int32 [16, 16], P('sp'), may hold values from 0 to 15, as said below
- counts: int32 [16], P('sp'), may hold values from 1 to 16, 128 in all
- offsets: int32 [2, 16], replicated, may hold values from 0 to 1384
- coupling: bfloat16 [40, 40], P('pb'), may hold values from -1 to 1
Outputs:
- residual: bfloat16 [40, 1024, 1024], P('pb', 'sp')
Inputs may be any that keep to these rules, and one draw needn't show every extreme that they name: `screened`: each row names 16 different blocks.
All inputs are finite; a program needn't handle non-finite values. No bound on the sum of `counts` on one device may be relied on, other than what follows from the above.
Results may differ from a plain program's by a relative error of at most 0.01.
Values may be sent and summed in bfloat16 or wider, within the bound.
No kernel may reach another device: no remote copies, remote signals or barrier semaphores. Data moves between devices by JAX's collectives and lax.ppermute only.
A program may use at most 64 MiB of HBM per device.

v0:
```python
import jax
import jax.numpy as jnp
from jax import lax
from jax.sharding import PartitionSpec as P

SHELL_ROW = 8
SHELL_COL = 16


def shards(amplitudes, virtuals, energies, integrals, screened, counts, offsets, coupling):
    pairs = amplitudes.shape[0]
    ext_rows = amplitudes.shape[1]
    width = SHELL_ROW * SHELL_COL
    nblk = lax.axis_size("sp")
    first = lax.axis_index("sp") * ext_rows
    local_cols = lax.dynamic_slice_in_dim(virtuals, first, ext_rows, 1)
    half = jnp.einsum(
        "pab,nb->pan", amplitudes, virtuals, preferred_element_type=jnp.float32
    ).astype(jnp.bfloat16)
    row_span = jnp.arange(SHELL_ROW, dtype=jnp.int32)
    col_span = jnp.arange(SHELL_COL, dtype=jnp.int32)
    lows = offsets[0]
    highs = offsets[1]
    left = local_cols[lows[:, None] + row_span[None, :]]
    right = half[:, :, highs[:, None] + col_span[None, :]]
    term = jnp.einsum("bia,pabs->bpis", left, right, preferred_element_type=jnp.float32)
    ao_all = lax.psum(term.reshape(nblk, pairs, width), "sp").astype(jnp.bfloat16)
    slots = screened.shape[1]
    live = (jnp.arange(slots, dtype=jnp.int32) < counts[0]).astype(jnp.bfloat16)
    chosen = jnp.take(ao_all, screened[0], axis=0) * live[:, None, None]
    slab = integrals.reshape(width, slots, width)
    raw = jnp.einsum("rkc,kpc->pr", slab, chosen, preferred_element_type=jnp.float32).astype(
        jnp.bfloat16
    )
    every = lax.all_gather(raw[None], ("sp", "pb"), axis=0, tiled=True)
    every = every.reshape(nblk, coupling.shape[1], width)
    k_all = jnp.einsum("pq,bqc->bpc", coupling, every, preferred_element_type=jnp.float32).astype(
        jnp.bfloat16
    )
    left_all = local_cols[offsets[0][:, None] + row_span[None, :]]
    right_rows = virtuals[offsets[1][:, None] + col_span[None, :]]
    square = k_all.reshape(nblk, pairs, SHELL_ROW, SHELL_COL)
    upper = jnp.einsum(
        "bia,bpis->pabs", left_all, square, preferred_element_type=jnp.float32
    ).astype(jnp.bfloat16)
    inner = jnp.einsum("pabs,bsn->pan", upper, right_rows, preferred_element_type=jnp.float32)
    own_energy = lax.dynamic_slice_in_dim(energies, first, ext_rows)
    diag = own_energy[:, None] + energies[None, :]
    return (inner + diag[None] * amplitudes.astype(jnp.float32)).astype(jnp.bfloat16)


def solution(mesh):
    return jax.shard_map(
        shards,
        mesh=mesh,
        in_specs=(
            P("pb", "sp", None),
            P(),
            P(),
            P("sp", None),
            P("sp", None),
            P("sp"),
            P(),
            P("pb", None),
        ),
        out_specs=P("pb", "sp", None),
        check_vma=False,
    )
```

profile of v0, /device:TPU:0, one launch (start us, length us, event | category | flops | bytes accessed | tf_op | source)
XLA Modules:
  0.0 168.3 jit_solution(11485403471382570395)
XLA Ops:
  0.0 1.8 %copy-done = bf16[1400,1024]{1,0:T(8,128)(2,1)S(1)} copy-done((bf16[1400,1024]{1,0:T(8,128)(2,1)S(1)}, bf16[1400,1024]{1,0:T(8,128)(2,1)}, u32[]{:S(2)}) %copy-start) | copy-done | bytes 2867224
  1.8 0.2 constant_dynamic-slice_fusion
  2.0 0.8 slice_bitcast_fusion
  2.7 0.1 compare_select_fusion
  2.8 0.1 reshape.178
  2.9 0.7 gather_fusion.1
  3.7 0.1 reshape.170
  3.8 7.6 %convolution_convert_fusion = bf16[20,64,1400]{2,1,0:T(8,128)(2,1)} fusion(bf16[20,64,1024]{2,1,0:T(8,128)(2,1)} %param.8, bf16[1400,1024]{1,0:T(8,128)(2,1)S(1)} %copy-done), kind=kOutput, calls=%fused_computation.6 | convolution fusion | flops 3671808000 | bytes 9072640 | tf_op jit(solution)/shard_map/pab,nb->pan/dot_general | solution.py:17
  11.4 10.8 %copy.25 = bf16[20,64,1400]{1,0,2:T(8,128)(2,1)} copy(bf16[20,64,1400]{2,1,0:T(8,128)(2,1)} %convolution_convert_fusion) | data formatting | bytes 7168000 | tf_op jit(solution)/shard_map/convert_element_type | solution.py:19
  22.2 5.5 %gather_fusion = bf16[256,20,64]{2,1,0:T(8,128)(2,1)} fusion(bf16[20,64,1400]{1,0,2:T(8,128)(2,1)} %copy.25, s32[1024]{0:T(1024)S(1)} %pad_clamp_fusion.2), kind=kCustom, calls=%fused_computation | custom fusion | bytes 1311744 | tf_op jit(solution)/shard_map/gather | solution.py:25
  27.6 5.1 %convolution_bitcast_fusion = f32[16,20,8,16]{1,2,3,0:T(8,128)} fusion(bf16[20,64,16,16]{1,0,3,2:T(8,128)(2,1)} %bitcast.75, bf16[128,64]{1,0:T(8,128)(2,1)S(1)} %gather_fusion.1), kind=kOutput, calls=%fused_computation.10 | convolution fusion | flops 5242880 | bytes 835584 | tf_op jit(solution)/shard_map/bia,pabs->bpis/dot_general | solution.py:26
  32.7 3.2 %copy.35 = f32[16,20,8,16]{3,2,1,0:T(8,128)} copy(f32[16,20,8,16]{1,2,3,0:T(8,128)} %convolution_bitcast_fusion) | data formatting | bytes 327680 | tf_op jit(solution)/shard_map/reshape | solution.py:27
  35.9 1.7 %reshape.214 = f32[16,20,128]{2,1,0:T(8,128)S(1)} reshape(f32[16,20,8,16]{3,2,1,0:T(8,128)} %copy.35) | data formatting | bytes 327680 | tf_op jit(solution)/shard_map/reshape | solution.py:27
  37.6 80.3 %all-reduce.1 = bf16[16,20,128]{2,1,0:T(8,128)(2,1)S(1)} all-reduce(f32[16,20,128]{2,1,0:T(8,128)S(1)} %reshape.214), channel_id=1, replica_groups=mesh['sp'=16,'pb'=2] {'sp'}, use_global_device_ids=true, to_apply=%region_0.0 | all-reduce | flops 40960 | bytes 245760 | tf_op jit(solution)/shard_map/psum | solution.py:27
  117.9 0.6 gather_fusion.2
  119.2 1.3 fusion.5
  120.5 36.9 %all-gather.1 = bf16[32,20,128]{2,1,0:T(8,128)(2,1)S(1)} all-gather(bf16[1,20,128]{2,1,0:T(8,128)(2,1)S(1)} %fusion.5), channel_id=2, replica_groups=mesh['sp'=16,'pb'=2] {'sp','pb'}, dimensions={0}, use_global_device_ids=true | all-gather | bytes 168960 | tf_op jit(solution)/shard_map/all_gather | solution.py:35
  157.4 0.2 fusion.3
  157.6 0.6 copy.31
  158.2 1.3 reshape.167
  159.6 0.8 dynamic_slice.7
  160.3 1.5 broadcast_add_fusion
  161.8 2.1 %gather_fusion.3 = bf16[256,1024]{1,0:T(8,128)(2,1)} fusion(bf16[1400,1024]{1,0:T(8,128)(2,1)S(1)} %copy-done, s32[1024]{0:T(1024)} %copy-done.1), kind=kCustom, calls=%fused_computation.3 | custom fusion | bytes 1049600 | tf_op jit(solution)/shard_map/gather | solution.py:41
  163.9 4.4 %fusion = bf16[20,64,1024]{2,1,0:T(8,128)(2,1)} fusion(bf16[20,64,1024]{2,1,0:T(8,128)(2,1)} %param.8, f32[64,1024]{1,0:T(8,128)} %broadcast_add_fusion, bf16[16,16,1024,1]{2,1,0,3:T(8,128)(2,1)} %bitcast.76, bf16[16,20,8,16]{3,2,0,1:T(8,128)(2,1)S(1)} %reshape.167, bf16[128,64]{1,0:T(8,128)(2,1)S(1)} %gather_fusion.1), kind=kOutput, calls=%fused_computation.5 | convolution fusion | flops 681902080 | bytes 6127616 | tf_op jit(solution)/shard_map/pabs,bsn->pan/dot_general | solution.py:46
  (14 shorter events, 0.2 us)
Async XLA Ops:
  0.0 1.8 %copy-start = (bf16[1400,1024]{1,0:T(8,128)(2,1)S(1)}, bf16[1400,1024]{1,0:T(8,128)(2,1)}, u32[]{:S(2)}) copy-start(bf16[1400,1024]{1,0:T(8,128)(2,1)} %param.9) | copy-start | bytes 8601604
  3.8 18.4 %copy-start.1 = (s32[1024]{0:T(1024)}, s32[1024]{0:T(1024)S(1)}, u32[]{:S(2)}) copy-start(s32[1024]{0:T(1024)S(1)} %pad_clamp_fusion.2) | copy-start | bytes 12292
  27.6 90.3 %copy-start.3 = (s32[1,16]{1,0:T(1,128)S(1)}, s32[1,16]{1,0:T(1,128)}, u32[]{:S(2)}) copy-start(s32[1,16]{1,0:T(1,128)} %param.12) | copy-start | bytes 196
  32.7 124.7 %copy-start.2 = (bf16[20,40]{1,0:T(8,128)(2,1)S(1)}, bf16[20,40]{1,0:T(8,128)(2,1)}, u32[]{:S(2)}) copy-start(bf16[20,40]{1,0:T(8,128)(2,1)} %param.15) | copy-start | bytes 4804
where the time goes:
time: 169 us; the launch traced here: 168 us
  blocking collectives  117 us (69%)
  local copies, waits for them, and re-layouts  30.2 us (18%)
  matrix products  18.6 us (11%)
    psum x1, blocking collectives, shards(): lax.psum(term.reshape(nblk, pairs, width), 'sp').astype(jnp.bfloat16)  80.3 us
    all_gather x1, blocking collectives, shards(): every = lax.all_gather(raw[None], ('sp', 'pb'), axis=0, tiled=True)  36.9 us
    convert_element_type x1, local copies, waits for them, and re-layouts, shards(): half = jnp.einsum('pab,nb->pan', amplitudes, virtuals, preferred_element_...  10.8 us
    dot_general x1, matrix products, shards(): jnp.einsum('pab,nb->pan', amplitudes, virtuals, preferred_element_type=jn...  7.57 us
    gather x1, local copies, waits for them, and re-layouts, shards(): right = half[:, :, highs[:, None] + col_span[None, :]]  5.49 us
    dot_general x1, matrix products, shards(): jnp.einsum('bia,pabs->bpis', left, right, preferred_element_type=jnp.floa...  5.06 us
    reshape x2, local copies, waits for them, and re-layouts, shards(): term.reshape(nblk, pairs, width)  4.85 us
    dot_general x1, matrix products, shards(): jnp.einsum('pabs,bsn->pan', upper, right_rows, preferred_element_type=jnp...  4.45 us

commit v1 on v0

--- a/solution.py
+++ b/solution.py
@@ -32,7 +32,10 @@
     raw = jnp.einsum("rkc,kpc->pr", slab, chosen, preferred_element_type=jnp.float32).astype(
         jnp.bfloat16
     )
-    every = lax.all_gather(raw[None], ("sp", "pb"), axis=0, tiled=True)
+    every = jnp.concatenate(
+        lax.all_to_all(jnp.stack([raw[None]] * lax.axis_size(("sp", "pb"))), ("sp", "pb"), 0, 0),
+        axis=0,
+    )
     every = every.reshape(nblk, coupling.shape[1], width)
     k_all = jnp.einsum("pq,bqc->bpc", coupling, every, preferred_element_type=jnp.float32).astype(
         jnp.bfloat16

time: 169 us -> 139 us (0.82)
  blocking collectives: 117 us -> 80.3 us
  waiting for transfers between devices: 0 us -> 6.14 us
  starting transfers between devices: 0 us -> 2.71 us
    all_gather x1 -> x0, blocking collectives: 36.9 us -> none  [shards(): every = lax.all_gather(raw[None], ('sp', 'pb'), axis=0, tiled=True)]
    all_to_all x0 -> x1, waiting for transfers between devices: none -> 6.14 us  [shards(): lax.all_to_all(jnp.stack([raw[None]] * lax.axis_size(('sp', 'pb'))), ('sp...]
    all_to_all x0 -> x1, starting transfers between devices: none -> 2.71 us  [shards(): lax.all_to_all(jnp.stack([raw[None]] * lax.axis_size(('sp', 'pb'))), ('sp...]
  transfers between devices with their start and end apart: 0 -> 1, of which waited for: 0 -> 1; matrix products, arithmetic and copies ran while one was open for 0% -> 2% of each run, Pallas kernels for 0% -> 0%
where the time goes in v1:
time: 139 us; the launch traced here: 138 us
  blocking collectives  80.3 us (58%)
  local copies, waits for them, and re-layouts  29 us (21%)
  matrix products  18.5 us (13%)
  waiting for transfers between devices  6.14 us (4%)
  starting transfers between devices  2.71 us (2%)
    psum x1, blocking collectives, shards(): lax.psum(term.reshape(nblk, pairs, width), 'sp').astype(jnp.bfloat16)  80.3 us
    convert_element_type x1, local copies, waits for them, and re-layouts, shards(): half = jnp.einsum('pab,nb->pan', amplitudes, virtuals, preferred_element_...  10.7 us
    dot_general x1, matrix products, shards(): jnp.einsum('pab,nb->pan', amplitudes, virtuals, preferred_element_type=jn...  7.47 us
    all_to_all x1, waiting for transfers between devices, shards(): lax.all_to_all(jnp.stack([raw[None]] * lax.axis_size(('sp', 'pb'))), ('sp...  6.14 us
    gather x1, local copies, waits for them, and re-layouts, shards(): right = half[:, :, highs[:, None] + col_span[None, :]]  5.49 us
    dot_general x1, matrix products, shards(): jnp.einsum('bia,pabs->bpis', left, right, preferred_element_type=jnp.floa...  5.07 us
    reshape x2, local copies, waits for them, and re-layouts, shards(): term.reshape(nblk, pairs, width)  4.84 us
    dot_general x1, matrix products, shards(): jnp.einsum('pabs,bsn->pan', upper, right_rows, preferred_element_type=jnp...  4.45 us
  transfers between devices with their start and end apart: 1, of which 1 were waited for; matrix products, arithmetic and copies ran while one was open for 2% of the time, Pallas kernels for 0%

profile of v1, /device:TPU:0, one launch (start us, length us, event | category | flops | bytes accessed | tf_op | source)
XLA Modules:
  0.0 138.3 jit_solution(8747100655846738503)
XLA Ops:
  0.0 0.8 slice_bitcast_fusion
  0.9 0.1 reshape.176
  1.1 0.1 reshape.168
  1.2 0.6 copy-done
  1.8 0.2 constant_dynamic-slice_fusion
  2.0 7.5 %convolution_convert_fusion = bf16[20,64,1400]{2,1,0:T(8,128)(2,1)} fusion(bf16[20,64,1024]{2,1,0:T(8,128)(2,1)} %param.8, bf16[1400,1024]{1,0:T(8,128)(2,1)S(1)} %copy-done), kind=kOutput, calls=%fused_computation.6 | convolution fusion | flops 3671808000 | bytes 9072640 | tf_op jit(solution)/shard_map/pab,nb->pan/dot_general | solution.py:17
  9.5 10.7 %copy.25 = bf16[20,64,1400]{1,0,2:T(8,128)(2,1)} copy(bf16[20,64,1400]{2,1,0:T(8,128)(2,1)} %convolution_convert_fusion) | data formatting | bytes 7168000 | tf_op jit(solution)/shard_map/convert_element_type | solution.py:19
  20.2 0.7 gather_fusion.1
  20.9 5.5 %gather_fusion = bf16[256,20,64]{2,1,0:T(8,128)(2,1)} fusion(bf16[20,64,1400]{1,0,2:T(8,128)(2,1)} %copy.25, s32[1024]{0:T(1024)S(1)} %pad_clamp_fusion.2), kind=kCustom, calls=%fused_computation | custom fusion | bytes 1311744 | tf_op jit(solution)/shard_map/gather | solution.py:25
  26.4 5.1 %convolution_bitcast_fusion = f32[16,20,8,16]{1,2,3,0:T(8,128)} fusion(bf16[20,64,16,16]{1,0,3,2:T(8,128)(2,1)} %bitcast.71, bf16[128,64]{1,0:T(8,128)(2,1)S(1)} %gather_fusion.1), kind=kOutput, calls=%fused_computation.10 | convolution fusion | flops 5242880 | bytes 835584 | tf_op jit(solution)/shard_map/bia,pabs->bpis/dot_general | solution.py:26
  31.5 3.2 %copy.35 = f32[16,20,8,16]{3,2,1,0:T(8,128)} copy(f32[16,20,8,16]{1,2,3,0:T(8,128)} %convolution_bitcast_fusion) | data formatting | bytes 327680 | tf_op jit(solution)/shard_map/reshape | solution.py:27
  34.7 1.7 %reshape.207 = f32[16,20,128]{2,1,0:T(8,128)S(1)} reshape(f32[16,20,8,16]{3,2,1,0:T(8,128)} %copy.35) | data formatting | bytes 327680 | tf_op jit(solution)/shard_map/reshape | solution.py:27
  36.3 80.3 %all-reduce.1 = bf16[16,20,128]{2,1,0:T(8,128)(2,1)S(1)} all-reduce(f32[16,20,128]{2,1,0:T(8,128)S(1)} %reshape.207), channel_id=1, replica_groups=mesh['sp'=16,'pb'=2] {'sp'}, use_global_device_ids=true, to_apply=%region_0.0 | all-reduce | flops 40960 | bytes 245760 | tf_op jit(solution)/shard_map/psum | solution.py:27
  117.4 0.6 gather_fusion.2
  118.0 1.3 fusion.4
  119.3 0.7 stack.3
  120.0 2.7 %all-to-all-start = ((bf16[32,1,20,128]{3,2,1,0:T(8,128)(2,1)}), bf16[32,1,20,128]{3,2,1,0:T(8,128)(2,1)S(1)}, u32[]{:S(2)}, u32[]{:S(2)}) async-start(bf16[32,1,20,128]{3,2,1,0:T(8,128)(2,1)} %stack.3), calls=%async_computation | async-start | bytes 393216 | tf_op jit(solution)/shard_map/all_to_all | solution.py:36
  122.8 2.0 %gather_fusion.3 = bf16[256,1024]{1,0:T(8,128)(2,1)} fusion(bf16[1400,1024]{1,0:T(8,128)(2,1)S(1)} %copy-done, s32[1024]{0:T(1024)S(1)} %pad_clamp_fusion.2), kind=kCustom, calls=%fused_computation.3 | custom fusion | bytes 1049600 | tf_op jit(solution)/shard_map/gather | solution.py:44
  124.8 0.8 broadcast_add_fusion
  125.6 6.1 %all-to-all-done = bf16[32,1,20,128]{3,2,1,0:T(8,128)(2,1)S(1)} async-done(((bf16[32,1,20,128]{3,2,1,0:T(8,128)(2,1)}), bf16[32,1,20,128]{3,2,1,0:T(8,128)(2,1)S(1)}, u32[]{:S(2)}, u32[]{:S(2)}) %all-to-all-start) | async-done | bytes 163872 | tf_op jit(solution)/shard_map/all_to_all | solution.py:36
  131.8 0.2 fusion.3
  131.9 0.6 copy.31
  132.6 1.3 reshape.165
  133.9 4.4 %fusion = bf16[20,64,1024]{2,1,0:T(8,128)(2,1)} fusion(bf16[20,64,1024]{2,1,0:T(8,128)(2,1)} %param.8, f32[64,1024]{1,0:T(8,128)} %broadcast_add_fusion, bf16[16,16,1024,1]{2,1,0,3:T(8,128)(2,1)} %bitcast.72, bf16[16,20,8,16]{3,2,0,1:T(8,128)(2,1)S(1)} %reshape.165, bf16[128,64]{1,0:T(8,128)(2,1)S(1)} %gather_fusion.1), kind=kOutput, calls=%fused_computation.5 | convolution fusion | flops 681902080 | bytes 6127616 | tf_op jit(solution)/shard_map/pabs,bsn->pan/dot_general | solution.py:49
  (16 shorter events, 0.3 us)
Async XLA Ops:
  0.0 1.8 %copy-start = (bf16[1400,1024]{1,0:T(8,128)(2,1)S(1)}, bf16[1400,1024]{1,0:T(8,128)(2,1)}, u32[]{:S(2)}) copy-start(bf16[1400,1024]{1,0:T(8,128)(2,1)} %param.9) | copy-start | bytes 8601604
  26.4 90.3 %copy-start.3 = (s32[1,16]{1,0:T(1,128)S(1)}, s32[1,16]{1,0:T(1,128)}, u32[]{:S(2)}) copy-start(s32[1,16]{1,0:T(1,128)} %param.12) | copy-start | bytes 196
  118.0 6.7 %copy-start.2 = (f32[1024]{0:T(1024)S(1)}, f32[1024]{0:T(1024)}, u32[]{:S(2)}) copy-start(f32[1024]{0:T(1024)} %param.10) | copy-start | bytes 12292
  120.0 11.7 %copy-start.1 = (bf16[20,40]{1,0:T(8,128)(2,1)S(1)}, bf16[20,40]{1,0:T(8,128)(2,1)}, u32[]{:S(2)}) copy-start(bf16[20,40]{1,0:T(8,128)(2,1)} %param.15) | copy-start | bytes 4804
  120.0 11.7 %all-to-all-start = ((bf16[32,1,20,128]{3,2,1,0:T(8,128)(2,1)}), bf16[32,1,20,128]{3,2,1,0:T(8,128)(2,1)S(1)}, u32[]{:S(2)}, u32[]{:S(2)}) async-start(bf16[32,1,20,128]{3,2,1,0:T(8,128)(2,1)} %stack.3), calls=%async_computation | async-start | bytes 393216 | tf_op jit(solution)/shard_map/all_to_all | solution.py:36
